TPU v7x, 32 devices: a whole 2x2x4 slice. The times are simulated.
32 devices in a mesh: dp: 4 (over x, core), ctx: 2 (over y), tensor: 4 (over z).
Axes of the slice: x: 2, y: 2, z: 4, core: 2. Of those that a mesh axis runs over, the one named last changes fastest.
Arguments:
- tokens: bfloat16 [4, 1024, 768], P('dp', 'ctx'), may hold values from -24 to 24
- lengths: int32 [4], P('dp'), may hold values from 128 to 1024, as said below
- cotangent: bfloat16 [4, 1024, 768], P('dp', 'ctx'), may hold values from -6 to 6
- qkv_weight: bfloat16 [3, 768, 768], P(None, 'dp', 'tensor'), may hold values from -0.21875 to 0.21875
- query_bias: float32 [768], P('tensor'), may hold values from -3 to 3
- value_bias: float32 [768], P('tensor'), may hold values from -0.18 to 0.18
- proj_weight: bfloat16 [768, 768], P('tensor', 'dp'), may hold values from -6 to 6
- proj_bias: float32 [768], replicated, may hold values from -2 to 2
- first_gain: float32 [768], replicated, may hold values from 0.1 to 1.9
- first_shift: float32 [768], replicated, may hold values from -2 to 2
- up_weight: bfloat16 [768, 3072], P('dp', 'tensor'), may hold values from -0.21875 to 0.21875
- up_bias: float32 [3072], P('tensor'), may hold values from -2 to 2
- down_weight: bfloat16 [3072, 768], P('tensor', 'dp'), may hold values from -0.109375 to 0.109375
- down_bias: float32 [768], replicated, may hold values from -2 to 2
- second_gain: float32 [768], replicated, may hold values from 0.1 to 1.9
- second_shift: float32 [768], replicated, may hold values from -2 to 2
Outputs:
- output: bfloat16 [4, 1024, 768], P('dp', 'ctx')
- grad_tokens: float32 [4, 1024, 768], P('dp', 'ctx')
- grad_qkv: float32 [3, 768, 768], P(None, 'dp', 'tensor')
- grad_query_bias: float32 [768], P('tensor')
- grad_value_bias: float32 [768], P('tensor')
- grad_proj: float32 [768, 768], P('tensor', 'dp')
- grad_proj_bias: float32 [768], replicated
- grad_first_gain: float32 [768], replicated
- grad_first_shift: float32 [768], replicated
- grad_up: float32 [768, 3072], P('dp', 'tensor')
- grad_up_bias: float32 [3072], P('tensor')
- grad_down: float32 [3072, 768], P('tensor', 'dp')
- grad_down_bias: float32 [768], replicated
- grad_second_gain: float32 [768], replicated
- grad_second_shift: float32 [768], replicated
Inputs may be any that keep to these rules, and one draw needn't show every extreme that they name: `lengths`: positions at or beyond a sequence's length are padding; they are still computed, but no position attends to them.
All inputs are finite; a program needn't handle non-finite values.
Results may differ from a plain program's by a relative error of at most 0.013.
The roundings to bfloat16 on the way count: a program that leaves them out, or rounds other values in their place, can miss the bound.
Values may be sent and summed in bfloat16 or wider, within the bound.
A program may use at most 128 MiB of HBM per device.

v0:
```python
import math
import jax
import jax.numpy as jnp
from jax import lax
from jax.sharding import PartitionSpec as P

HD = 64
EPSILON = 1e-05
NEGATIVE = -1e30
ROOT_HALF = 0.7071067811865476
ROOT_TWO_PI = 2.5066282746310002


def layer_norm(hidden_in, norm_gain, norm_shift):
    centred = hidden_in - jnp.mean(hidden_in, axis=-1, keepdims=True)
    inverse = lax.rsqrt(jnp.mean(centred * centred, axis=-1, keepdims=True) + EPSILON)
    normed = centred * inverse
    return (normed * norm_gain + norm_shift, normed, inverse)


def norm_back(upstream, normed, inverse, norm_gain):
    scaled = upstream * norm_gain
    return inverse * (
        scaled
        - jnp.mean(scaled, axis=-1, keepdims=True)
        - normed * jnp.mean(scaled * normed, axis=-1, keepdims=True)
    )


def gelu_value(pre_act):
    return 0.5 * pre_act * (1.0 + jax.scipy.special.erf(pre_act * ROOT_HALF))


def gelu_slope(pre_act):
    return (
        0.5 * (1.0 + jax.scipy.special.erf(pre_act * ROOT_HALF))
        + pre_act * jnp.exp(-0.5 * pre_act * pre_act) / ROOT_TWO_PI
    )


def attend_piece(running, pieces, queries, length, score_scale):
    key_piece, value_piece = pieces
    piece_rows = key_piece.shape[0]
    block_width = math.gcd(piece_rows, 512)
    block_count = piece_rows // block_width
    heads_here = key_piece.shape[1]
    key_blocks = key_piece.reshape(block_count, block_width, heads_here, HD)
    value_blocks = value_piece.reshape(block_count, block_width, heads_here, HD)

    def one_block(carried, block_item):
        run_max, run_total, run_acc = carried
        key_block, value_block, block_index = block_item
        positions = block_index * block_width + jnp.arange(block_width, dtype=jnp.int32)
        key_mask = (positions < length)[None, None, :]
        scores = (
            jnp.einsum("qhe,khe->hqk", queries, key_block, preferred_element_type=jnp.float32)
            * score_scale
        )
        scores = jnp.where(key_mask, scores, NEGATIVE)
        new_max = jnp.maximum(run_max, jnp.max(scores, axis=-1))
        rescale = jnp.exp(run_max - new_max)
        weights_now = jnp.where(key_mask, jnp.exp(scores - new_max[..., None]), 0.0)
        run_total = run_total * rescale + jnp.sum(weights_now, axis=-1)
        run_acc = run_acc * rescale.T[..., None] + jnp.einsum(
            "hqk,khe->qhe",
            weights_now.astype(jnp.bfloat16),
            value_block,
            preferred_element_type=jnp.float32,
        )
        return ((new_max, run_total, run_acc), None)

    block_numbers = jnp.arange(block_count, dtype=jnp.int32)
    carried, unused = lax.scan(one_block, running, (key_blocks, value_blocks, block_numbers))
    return carried


def per_device(
    tokens,
    lengths,
    cotangent,
    qkv_weight,
    query_bias,
    value_bias,
    proj_weight,
    proj_bias,
    first_gain,
    first_shift,
    up_weight,
    up_bias,
    down_weight,
    down_bias,
    second_gain,
    second_shift,
):
    wide_qkv, wide_proj, wide_up, wide_down = (
        lax.all_gather(qkv_weight, "dp", axis=1, tiled=True),
        lax.all_gather(proj_weight, "dp", axis=1, tiled=True),
        lax.all_gather(up_weight, "dp", axis=0, tiled=True),
        lax.all_gather(down_weight, "dp", axis=1, tiled=True),
    )
    rows_in = tokens[0]
    length = lengths[0]
    row_count = rows_in.shape[0]
    local_width = wide_qkv.shape[2]
    heads_here = local_width // HD
    score_scale = 1.0 / math.sqrt(HD)
    projected = jnp.einsum("td,ide->ite", rows_in, wide_qkv, preferred_element_type=jnp.float32)
    queries = (projected[0] + query_bias).astype(jnp.bfloat16).reshape(row_count, heads_here, HD)
    key_rows = projected[1].astype(jnp.bfloat16).reshape(row_count, heads_here, HD)
    value_rows = (projected[2] + value_bias).astype(jnp.bfloat16).reshape(row_count, heads_here, HD)
    initial = (
        jnp.full((heads_here, row_count), NEGATIVE, jnp.float32),
        jnp.zeros((heads_here, row_count), jnp.float32),
        jnp.zeros((row_count, heads_here, HD), jnp.float32),
    )
    run_max, run_total, run_acc = attend_piece(
        initial,
        (
            lax.all_gather(key_rows, "ctx", axis=0, tiled=True),
            lax.all_gather(value_rows, "ctx", axis=0, tiled=True),
        ),
        queries,
        length,
        score_scale,
    )
    attended = run_acc / run_total.T[..., None]
    log_total = run_max + jnp.log(run_total)
    attended_low = attended.reshape(row_count, local_width).astype(jnp.bfloat16)
    attn_part = jnp.dot(attended_low, wide_proj, preferred_element_type=jnp.float32)
    first_sum = rows_in.astype(jnp.float32) + lax.psum(attn_part, "tensor") + proj_bias
    first_out, first_normed, first_inverse = layer_norm(first_sum, first_gain, first_shift)
    first_low = first_out.astype(jnp.bfloat16)
    pre_act = jnp.dot(first_low, wide_up, preferred_element_type=jnp.float32) + up_bias
    hidden = gelu_value(pre_act).astype(jnp.bfloat16)
    down_part = jnp.dot(hidden, wide_down, preferred_element_type=jnp.float32)
    second_sum = first_out + lax.psum(down_part, "tensor") + down_bias
    result, second_normed, second_inverse = layer_norm(second_sum, second_gain, second_shift)
    output = result.astype(jnp.bfloat16)[None]
    upstream = cotangent[0].astype(jnp.float32)
    grad_second_shift = jnp.sum(upstream, axis=0)
    grad_second_gain = jnp.sum(upstream * second_normed, axis=0)
    d_second = norm_back(upstream, second_normed, second_inverse, second_gain)
    grad_down_bias = jnp.sum(d_second, axis=0)
    d_second_low = d_second.astype(jnp.bfloat16)
    grad_down = jnp.einsum("tf,td->fd", hidden, d_second_low, preferred_element_type=jnp.float32)
    d_hidden = jnp.einsum("td,fd->tf", d_second_low, wide_down, preferred_element_type=jnp.float32)
    d_pre = d_hidden * gelu_slope(pre_act)
    grad_up_bias = jnp.sum(d_pre, axis=0)
    d_pre_low = d_pre.astype(jnp.bfloat16)
    grad_up = jnp.einsum("td,tf->df", first_low, d_pre_low, preferred_element_type=jnp.float32)
    first_part = jnp.einsum("tf,df->td", d_pre_low, wide_up, preferred_element_type=jnp.float32)
    d_first = lax.psum(first_part, "tensor") + d_second
    grad_first_shift = jnp.sum(d_first, axis=0)
    grad_first_gain = jnp.sum(d_first * first_normed, axis=0)
    d_attn = norm_back(d_first, first_normed, first_inverse, first_gain)
    grad_proj_bias = jnp.sum(d_attn, axis=0)
    d_attn_low = d_attn.astype(jnp.bfloat16)
    grad_proj = jnp.einsum(
        "te,td->ed", attended_low, d_attn_low, preferred_element_type=jnp.float32
    )
    d_heads = jnp.einsum("td,ed->te", d_attn_low, wide_proj, preferred_element_type=jnp.float32)
    d_heads = d_heads.astype(jnp.bfloat16).reshape(row_count, heads_here, HD)
    row_delta = jnp.sum(d_heads.astype(jnp.float32) * attended, axis=-1).T
    key_back, value_back = (
        lax.all_gather(key_rows, "ctx", axis=0, tiled=True),
        lax.all_gather(value_rows, "ctx", axis=0, tiled=True),
    )
    seq_rows = key_back.shape[0]
    block_width = math.gcd(seq_rows, 512)
    block_count = seq_rows // block_width

    def back_block(d_query, block_item):
        key_block, value_block, block_index = block_item
        positions = block_index * block_width + jnp.arange(block_width, dtype=jnp.int32)
        key_mask = (positions < length)[None, None, :]
        scores = (
            jnp.einsum("qhe,khe->hqk", queries, key_block, preferred_element_type=jnp.float32)
            * score_scale
        )
        scores = jnp.where(key_mask, scores, NEGATIVE)
        probabilities = jnp.where(key_mask, jnp.exp(scores - log_total[..., None]), 0.0)
        probs_low = probabilities.astype(jnp.bfloat16)
        value_grad = jnp.einsum(
            "hqk,qhe->khe", probs_low, d_heads, preferred_element_type=jnp.float32
        )
        d_probs = jnp.einsum(
            "qhe,khe->hqk", d_heads, value_block, preferred_element_type=jnp.float32
        )
        d_scores = (probabilities * (d_probs - row_delta[..., None])).astype(jnp.bfloat16)
        d_query = (
            d_query
            + jnp.einsum("hqk,khe->qhe", d_scores, key_block, preferred_element_type=jnp.float32)
            * score_scale
        )
        key_grad = (
            jnp.einsum("hqk,qhe->khe", d_scores, queries, preferred_element_type=jnp.float32)
            * score_scale
        )
        return (d_query, (key_grad, value_grad))

    block_items = (
        key_back.reshape(block_count, block_width, heads_here, HD),
        value_back.reshape(block_count, block_width, heads_here, HD),
        jnp.arange(block_count, dtype=jnp.int32),
    )
    d_query, (key_grads, value_grads) = lax.scan(
        back_block, jnp.zeros((row_count, heads_here, HD), jnp.float32), block_items
    )
    key_grads = key_grads.reshape(seq_rows, heads_here, HD)
    value_grads = value_grads.reshape(seq_rows, heads_here, HD)
    own_keys, own_values = (
        lax.psum_scatter(key_grads, "ctx", scatter_dimension=0, tiled=True),
        lax.psum_scatter(value_grads, "ctx", scatter_dimension=0, tiled=True),
    )
    query_flat = d_query.reshape(row_count, local_width)
    key_flat = own_keys.reshape(row_count, local_width)
    value_flat = own_values.reshape(row_count, local_width)
    grad_query_bias = jnp.sum(query_flat, axis=0)
    grad_value_bias = jnp.sum(value_flat, axis=0)
    d_stack = jnp.stack(
        [
            query_flat.astype(jnp.bfloat16),
            key_flat.astype(jnp.bfloat16),
            value_flat.astype(jnp.bfloat16),
        ]
    )
    grad_qkv = jnp.einsum("td,ite->ide", rows_in, d_stack, preferred_element_type=jnp.float32)
    input_part = jnp.einsum("ite,ide->td", d_stack, wide_qkv, preferred_element_type=jnp.float32)
    grad_tokens = (d_attn + lax.psum(input_part, "tensor"))[None]
    local_grads = (grad_qkv, grad_proj, grad_up, grad_down)
    grad_pieces = (
        lax.psum_scatter(local_grads[0], ("dp", "ctx"), scatter_dimension=1, tiled=True),
        lax.psum_scatter(local_grads[1], ("dp", "ctx"), scatter_dimension=1, tiled=True),
        lax.psum_scatter(local_grads[2], ("dp", "ctx"), scatter_dimension=0, tiled=True),
        lax.psum_scatter(local_grads[3], ("dp", "ctx"), scatter_dimension=1, tiled=True),
    )
    owned_grads = (
        lax.all_gather(grad_pieces[0], "ctx", axis=1, tiled=True),
        lax.all_gather(grad_pieces[1], "ctx", axis=1, tiled=True),
        lax.all_gather(grad_pieces[2], "ctx", axis=0, tiled=True),
        lax.all_gather(grad_pieces[3], "ctx", axis=1, tiled=True),
    )
    vector_grads = lax.psum(
        (
            grad_query_bias,
            grad_value_bias,
            grad_proj_bias,
            grad_first_gain,
            grad_first_shift,
            grad_up_bias,
            grad_down_bias,
            grad_second_gain,
            grad_second_shift,
        ),
        ("dp", "ctx"),
    )
    return (
        output,
        grad_tokens,
        owned_grads[0],
        vector_grads[0],
        vector_grads[1],
        owned_grads[1],
        vector_grads[2],
        vector_grads[3],
        vector_grads[4],
        owned_grads[2],
        vector_grads[5],
        owned_grads[3],
        vector_grads[6],
        vector_grads[7],
        vector_grads[8],
    )


def solution(mesh):
    placed = (
        P("dp", "ctx", None),
        P("dp"),
        P("dp", "ctx", None),
        P(None, "dp", "tensor"),
        P("tensor"),
        P("tensor"),
        P("tensor", "dp"),
        P(),
        P(),
        P(),
        P("dp", "tensor"),
        P("tensor"),
        P("tensor", "dp"),
        P(),
        P(),
        P(),
    )
    return jax.shard_map(
        per_device,
        mesh=mesh,
        in_specs=placed,
        out_specs=(
            P("dp", "ctx", None),
            P("dp", "ctx", None),
            P(None, "dp", "tensor"),
            P("tensor"),
            P("tensor"),
            P("tensor", "dp"),
            P(),
            P(),
            P(),
            P("dp", "tensor"),
            P("tensor"),
            P("tensor", "dp"),
            P(),
            P(),
            P(),
        ),
        check_vma=False,
    )
```

profile of v0, /device:TPU:0, one launch (start us, length us, event | category | flops | bytes accessed | tf_op | source)
XLA Modules:
  0.0 575.8 jit_solution(4283684153634687425)
XLA Ops:
  9.4 14.3 %all_gather.32 = bf16[3,768,192]{2,0,1:T(4,128)(2,1)S(1)} all-gather(bf16[3,192,192]{2,0,1:T(4,128)(2,1)S(1)} %copy.46), channel_id=1, replica_groups=mesh['dp'=4,'ctx'=2,'tensor'=4] {'dp'}, dimensions={1}, use_global_device_ids=true | all-gather | bytes 1105920 | tf_op jit(solution)/shard_map/all_gather | solution.py:96
  25.9 6.6 %all_gather.35 = bf16[192,768]{0,1:T(8,128)(2,1)S(1)} all-gather(bf16[192,192]{0,1:T(8,128)(2,1)S(1)} %copy.50), channel_id=1, replica_groups=mesh['dp'=4,'ctx'=2,'tensor'=4] {'dp'}, dimensions={1}, use_global_device_ids=true | all-gather | bytes 368640 | tf_op jit(solution)/shard_map/all_gather | solution.py:97
  32.5 7.8 %all_gather.33 = bf16[1024,3,64]{0,2,1:T(8,128)(2,1)S(1)} all-gather(bf16[512,3,64]{0,2,1:T(8,128)(2,1)S(1)} %bitcast.194), channel_id=1, replica_groups=mesh['dp'=4,'ctx'=2,'tensor'=4] {'ctx'}, dimensions={0}, use_global_device_ids=true | all-gather | bytes 589824 | tf_op jit(solution)/shard_map/all_gather | solution.py:119
  40.4 7.0 %all_gather.34 = bf16[1024,3,64]{0,2,1:T(8,128)(2,1)S(1)} all-gather(bf16[512,3,64]{0,2,1:T(8,128)(2,1)S(1)} %add_convert_fusion.1), channel_id=1, replica_groups=mesh['dp'=4,'ctx'=2,'tensor'=4] {'ctx'}, dimensions={0}, use_global_device_ids=true | all-gather | bytes 589824 | tf_op jit(solution)/shard_map/all_gather | solution.py:120
  47.5 9.2 %while.30 = (s32[]{:T(128)}, f32[3,512]{1,0:T(4,128)S(1)}, f32[3,512]{1,0:T(4,128)S(1)}, f32[512,3,64]{0,2,1:T(8,128)S(1)}, s32[2]{0:T(128)S(1)}, /*index=5*/s32...) while((s32[]{:T(128)}, f32[3,512]{1,0:T(4,128)S(1)}, ...), condition=%wide.region_3.4_spmd.clone, body=%wide.region_0.3_spmd.clone.sunk | while | flops 211855360 | bytes 10918577 | solution.py:73
  59.6 68.7 %all-reduce.6.cloned.1.call-done = f32[512,768]{1,0:T(8,128)} async-done(((f32[512,768]{1,0:T(8,128)}), f32[512,768]{1,0:T(8,128)}) %all-reduce.6.cloned.1.call-update) | async-done | bytes 1572880 | tf_op jit(solution)/shard_map/psum | solution.py:130
  131.0 3.7 multiply_convert_fusion.1
  138.2 68.2 %all-reduce.8.cloned.1.call-done = f32[512,768]{1,0:T(8,128)} async-done(((f32[512,768]{1,0:T(8,128)}), f32[512,768]{1,0:T(8,128)}) %all-reduce.8.cloned.1.call-update) | async-done | bytes 1572880 | tf_op jit(solution)/shard_map/psum | solution.py:136
  218.5 67.4 %all-reduce.10.cloned.1.call-done = f32[512,768]{1,0:T(8,128)} async-done(((f32[512,768]{1,0:T(8,128)}), f32[512,768]{1,0:T(8,128)}) %all-reduce.10.cloned.1.call-update) | async-done | bytes 1572880 | tf_op jit(solution)/shard_map/psum | solution.py:152
  293.2 48.6 %while.31 = (s32[]{:T(128)}, f32[512,3,64]{0,2,1:T(8,128)S(1)}, f32[2,512,3,64]{1,0,3,2:T(2,128)}, f32[2,512,3,64]{1,0,3,2:T(2,128)}, bf16[2,512,3,64]{1,3,2,0:T...) while((s32[]{:T(128)}, f32[512,3,64]{0,2,1:T(8,128)S(1)}, ...), condition=%wide.region_17.18_spmd.clone, body=%wide.region_16.17_spmd.clone.sunk | while | flops 513147904 | bytes 22656808 | solution.py:206
  301.4 8.0 %dynamic_update_slice.11 = f32[2,512,3,64]{1,0,3,2:T(2,128)} dynamic-update-slice(f32[2,512,3,64]{1,0,3,2:T(2,128)} %get-tuple-element.565, f32[1,512,3,64]{1,0,3,2:T(1,128)S(1)} %copy.99, s32[]{:T(128)S(6)} %copy.122, s32[]{:T(128)} %constant.61.clone.1..sunk.1, s32[]{:T(128)} %constant.61.clone.1..sunk.1, s32[]{:T(128)} %constant.61.clone.1..sunk.1) | dynamic-update-slice | bytes 786436 | tf_op jit(solution)/shard_map/while/body/jit(dynamic_update_index_in_dim)/dynamic_update_slice | solution.py:206
  309.4 8.0 %dynamic_update_slice.12 = f32[2,512,3,64]{1,0,3,2:T(2,128)} dynamic-update-slice(f32[2,512,3,64]{1,0,3,2:T(2,128)} %get-tuple-element.566, f32[1,512,3,64]{1,0,3,2:T(1,128)S(1)} %copy.100, s32[]{:T(128)S(6)} %copy.122, s32[]{:T(128)} %constant.61.clone.1..sunk.1, s32[]{:T(128)} %constant.61.clone.1..sunk.1, s32[]{:T(128)} %constant.61.clone.1..sunk.1) | dynamic-update-slice | bytes 786436 | tf_op jit(solution)/shard_map/while/body/jit(dynamic_update_index_in_dim)/dynamic_update_slice | solution.py:206
  325.7 8.0 %dynamic_update_slice.11 = f32[2,512,3,64]{1,0,3,2:T(2,128)} dynamic-update-slice(f32[2,512,3,64]{1,0,3,2:T(2,128)} %get-tuple-element.565, f32[1,512,3,64]{1,0,3,2:T(1,128)S(1)} %copy.99, s32[]{:T(128)S(6)} %copy.122, s32[]{:T(128)} %constant.61.clone.1..sunk.1, s32[]{:T(128)} %constant.61.clone.1..sunk.1, s32[]{:T(128)} %constant.61.clone.1..sunk.1) | dynamic-update-slice | bytes 786436 | tf_op jit(solution)/shard_map/while/body/jit(dynamic_update_index_in_dim)/dynamic_update_slice | solution.py:206
  333.7 8.0 %dynamic_update_slice.12 = f32[2,512,3,64]{1,0,3,2:T(2,128)} dynamic-update-slice(f32[2,512,3,64]{1,0,3,2:T(2,128)} %get-tuple-element.566, f32[1,512,3,64]{1,0,3,2:T(1,128)S(1)} %copy.100, s32[]{:T(128)S(6)} %copy.122, s32[]{:T(128)} %constant.61.clone.1..sunk.1, s32[]{:T(128)} %constant.61.clone.1..sunk.1, s32[]{:T(128)} %constant.61.clone.1..sunk.1) | dynamic-update-slice | bytes 786436 | tf_op jit(solution)/shard_map/while/body/jit(dynamic_update_index_in_dim)/dynamic_update_slice | solution.py:206
  362.2 18.7 %reduce-scatter.13.cloned.1.call-done = f32[512,3,64]{0,2,1:T(8,128)} async-done(((f32[1024,3,64]{0,2,1:T(8,128)}), f32[512,3,64]{0,2,1:T(8,128)}) %reduce-scatter.13.cloned.1.call-update) | async-done | bytes 393232 | tf_op jit(solution)/shard_map/reduce_scatter | solution.py:213
  394.4 24.5 %reduce-scatter.21.cloned.1.call-done = f32[96,192]{1,0:T(8,128)} async-done(((f32[768,192]{1,0:T(8,128)}), f32[96,192]{1,0:T(8,128)}) %reduce-scatter.21.cloned.1.call-update) | async-done | bytes 73744
  419.0 5.5 all_gather.39
  425.4 26.3 %all-reduce = (f32[192]{0:T(256)}, f32[192]{0:T(256)}, f32[768]{0:T(1024)}, f32[768]{0:T(1024)}, f32[768]{0:T(1024)}, /*index=5*/f32[768]{0:T(1024)}, f32[768]{0:T(1024)}, f32[768]{0:T(1024)}, f32[768]{0:T(1024)}) all-reduce(f32[192]{0:T(256)S(1)} %reduce_sum.185, ...), channel_id=1, replica_groups=mesh['dp'=4,'ctx'=2,'tensor'=4] {'dp','ctx'}, use_global_device_ids=true, to_apply=%region_23.24 | all-reduce | flops 5760 | bytes 46080 | tf_op jit(solution)/shard_map/psum | solution.py:243
  451.6 13.2 %reduce-scatter.15.cloned.1.call-done = f32[96,768]{1,0:T(8,128)} async-done(((f32[768,768]{1,0:T(8,128)}), f32[96,768]{1,0:T(8,128)}) %reduce-scatter.15.cloned.1.call-update) | async-done | bytes 294928 | tf_op jit(solution)/shard_map/reduce_scatter | solution.py:234
  464.9 9.4 %all_gather.40 = f32[192,768]{1,0:T(8,128)S(1)} all-gather(f32[96,768]{1,0:T(8,128)} %reduce-scatter.15.cloned.1.call-done), channel_id=1, replica_groups=mesh['dp'=4,'ctx'=2,'tensor'=4] {'ctx'}, dimensions={0}, use_global_device_ids=true | all-gather | bytes 884736 | tf_op jit(solution)/shard_map/all_gather | solution.py:240
  474.2 36.1 %reduce-scatter.17.cloned.1.call-done = f32[768,96]{0,1:T(8,128)} async-done(((f32[768,768]{0,1:T(8,128)}), f32[768,96]{0,1:T(8,128)}) %reduce-scatter.17.cloned.1.call-update) | async-done | bytes 294928 | tf_op jit(solution)/shard_map/reduce_scatter | solution.py:235
  510.3 9.4 %all_gather.41 = f32[768,192]{0,1:T(8,128)S(1)} all-gather(f32[768,96]{0,1:T(8,128)} %reduce-scatter.17.cloned.1.call-done), channel_id=1, replica_groups=mesh['dp'=4,'ctx'=2,'tensor'=4] {'ctx'}, dimensions={1}, use_global_device_ids=true | all-gather | bytes 884736 | tf_op jit(solution)/shard_map/all_gather | solution.py:241
  522.5 31.1 %reduce-scatter.19.cloned.1.call-done = f32[96,576]{1,0:T(8,128)} async-done(((f32[768,576]{1,0:T(8,128)}), f32[96,576]{1,0:T(8,128)}) %reduce-scatter.19.cloned.1.call-update) | async-done | bytes 221200
  554.8 11.3 %all_gather.38 = f32[3,192,192]{2,0,1:T(4,128)S(1)} all-gather(f32[3,96,192]{2,0,1:T(4,128)S(1)} %bitcast.191), channel_id=1, replica_groups=mesh['dp'=4,'ctx'=2,'tensor'=4] {'ctx'}, dimensions={1}, use_global_device_ids=true | all-gather | bytes 663552 | tf_op jit(solution)/shard_map/all_gather | solution.py:238
  (217 shorter events, 96.0 us)
Async XLA Ops:
  8.0 120.3 %all-reduce.6.cloned.1.call-start = ((), (), s32[]{:S(2)}) async-start(), calls=%async_computation.6 | async-start | bytes 3145728 | tf_op jit(solution)/shard_map/psum | solution.py:130
  58.4 70.0 %copy-start.31 = (f32[768]{0:T(1024)S(1)}, f32[768]{0:T(1024)}, u32[]{:S(2)}) copy-start(f32[768]{0:T(1024)} %param.27) | copy-start | bytes 9220
  58.4 72.2 %all-gather.3.cloned.1.call-start = ((), (), s32[]{:S(2)}) async-start(), calls=%async_computation.7 | async-start | bytes 1474560 | tf_op jit(solution)/shard_map/all_gather | solution.py:98
  59.0 75.7 %all-gather.5.cloned.1.call-start = ((), (), s32[]{:S(2)}) async-start(), calls=%async_computation.8 | async-start | bytes 1474560 | tf_op jit(solution)/shard_map/all_gather | solution.py:99
  59.6 146.9 %all-reduce.8.cloned.1.call-start = ((), (), s32[]{:S(2)}) async-start(), calls=%async_computation.9 | async-start | bytes 3145728 | tf_op jit(solution)/shard_map/psum | solution.py:136
  130.3 76.2 %copy-start.16 = (f32[512]{0:T(512)}, f32[512]{0:T(512)S(1)}, u32[]{:S(2)}) copy-start(f32[512]{0:T(512)S(1)} %broadcast_multiply_fusion.5) | copy-start | bytes 6148
  130.6 75.8 %copy-start.20 = (f32[512]{0:T(512)}, f32[512]{0:T(512)S(1)}, u32[]{:S(2)}) copy-start(f32[512]{0:T(512)S(1)} %add_rsqrt_fusion.1) | copy-start | bytes 6148
  138.1 68.3 %copy-start.32 = (f32[768]{0:T(1024)S(1)}, f32[768]{0:T(1024)}, u32[]{:S(2)}) copy-start(f32[768]{0:T(1024)} %param.33) | copy-start | bytes 9220
  138.2 147.7 %all-reduce.10.cloned.1.call-start = ((), (), s32[]{:S(2)}) async-start(), calls=%async_computation.10 | async-start | bytes 3145728 | tf_op jit(solution)/shard_map/psum | solution.py:152
  217.6 143.5 %reduce-scatter.11.cloned.1.call-start = ((), (), s32[]{:S(2)}) async-start(), calls=%async_computation.11 | async-start | bytes 1179648 | tf_op jit(solution)/shard_map/reduce_scatter | solution.py:212
  218.5 70.8 %copy-start.17 = (f32[512]{0:T(512)S(1)}, f32[512]{0:T(512)}, u32[]{:S(2)}) copy-start(f32[512]{0:T(512)} %copy-done.16) | copy-start | bytes 6148
  218.5 70.8 %copy-start.19 = (f32[768]{0:T(1024)S(1)}, f32[768]{0:T(1024)}, u32[]{:S(2)}) copy-start(f32[768]{0:T(1024)} %param.28) | copy-start | bytes 9220
  344.4 36.4 %reduce-scatter.13.cloned.1.call-start = ((), (), s32[]{:S(2)}) async-start(), calls=%async_computation.12 | async-start | bytes 1179648 | tf_op jit(solution)/shard_map/reduce_scatter | solution.py:213
  347.3 71.7 %reduce-scatter.21.cloned.1.call-start = ((), (), s32[]{:S(2)}) async-start(), calls=%async_computation.17 | async-start | bytes 884736
  350.1 114.8 %reduce-scatter.15.cloned.1.call-start = ((), (), s32[]{:S(2)}) async-start(), calls=%async_computation.14 | async-start | bytes 2654208 | tf_op jit(solution)/shard_map/reduce_scatter | solution.py:234
  353.8 156.5 %reduce-scatter.17.cloned.1.call-start = ((), (), s32[]{:S(2)}) async-start(), calls=%async_computation.15 | async-start | bytes 2654208 | tf_op jit(solution)/shard_map/reduce_scatter | solution.py:235
  357.6 162.1 %all-reduce.12.cloned.1.call-start = ((), (), s32[]{:S(2)}) async-start(), calls=%async_computation.13 | async-start | bytes 3145728 | tf_op jit(solution)/shard_map/psum | solution.py:229
  384.2 169.4 %reduce-scatter.19.cloned.1.call-start = ((), (), s32[]{:S(2)}) async-start(), calls=%async_computation.16 | async-start | bytes 2211840
  393.0 32.3 %copy-start.23 = (f32[768]{0:T(1024)S(1)}, f32[768]{0:T(1024)}, u32[]{:S(2)}) copy-start(f32[768]{0:T(1024)} %get-tuple-element.292) | copy-start | bytes 9220
  393.0 32.3 %copy-start.24 = (f32[768]{0:T(1024)S(1)}, f32[768]{0:T(1024)}, u32[]{:S(2)}) copy-start(f32[768]{0:T(1024)} %get-tuple-element.352) | copy-start | bytes 9220
  393.1 32.3 %copy-start.26 = (f32[768]{0:T(1024)S(1)}, f32[768]{0:T(1024)}, u32[]{:S(2)}) copy-start(f32[768]{0:T(1024)} %get-tuple-element.350) | copy-start | bytes 9220
  393.1 32.3 %copy-start.27 = (f32[768]{0:T(1024)S(1)}, f32[768]{0:T(1024)}, u32[]{:S(2)}) copy-start(f32[768]{0:T(1024)} %get-tuple-element.290) | copy-start | bytes 9220
  393.1 32.3 %copy-start.28 = (f32[768]{0:T(1024)S(1)}, f32[768]{0:T(1024)}, u32[]{:S(2)}) copy-start(f32[768]{0:T(1024)} %get-tuple-element.295) | copy-start | bytes 9220
  394.2 125.5 %copy-start.1 = (f32[512,768]{1,0:T(8,128)S(1)}, f32[512,768]{1,0:T(8,128)}, u32[]{:S(2)}) copy-start(f32[512,768]{1,0:T(8,128)} %copy-done) | copy-start | bytes 4718596
  (34 other events, 116.1 us)
Sparse Core Ops, SparseCore 0:
  58.5 69.7 all-reduce.5
  138.3 68.1 all-reduce.7
  217.7 68.1 all-reduce.9
  384.4 68.9 all-reduce.11
Sparse Core Ops, SparseCore 1:
  60.4 18.1 all-gather.2
  80.0 17.3 all-gather.4
  344.5 16.6 reduce-scatter.10
  363.4 17.4 reduce-scatter.12
  384.0 34.9 reduce-scatter.20
  422.3 42.5 reduce-scatter.14
  468.1 42.2 reduce-scatter.16
  513.6 40.0 reduce-scatter.18
where the time goes:
time: 579 us; the launch traced here: 576 us
  waiting for transfers between devices  333 us (58%)
  blocking collectives  97.5 us (17%)
  local copies, waits for them, and re-layouts  63.7 us (11%)
  matrix products  38.8 us (7%)
  other arithmetic  23.7 us (4%)
  between operations  15.8 us (3%)
    psum x1, waiting for transfers between devices, per_device(): lax.psum(attn_part, 'tensor')  68.7 us
    psum x1, waiting for transfers between devices, per_device(): second_sum = first_out + lax.psum(down_part, 'tensor') + down_bias  68.2 us
    psum x1, waiting for transfers between devices, per_device(): d_first = lax.psum(first_part, 'tensor') + d_second  67.4 us
    unnamed x14, waiting for transfers between devices  56.9 us
    reduce_scatter x1, waiting for transfers between devices, per_device(): lax.psum_scatter(local_grads[3], ('dp', 'ctx'), scatter_dimension=1, tile...  36.1 us
    dynamic_update_slice x8, local copies, waits for them, and re-layouts, per_device(): lax.scan(back_block, jnp.zeros((row_count, heads_here, HD), jnp.float32),...  33.7 us
    psum x1, blocking collectives, per_device(): lax.psum((grad_query_bias, grad_value_bias, grad_proj_bias, grad_first_ga...  26.3 us
    unnamed x89, local copies, waits for them, and re-layouts  19.3 us
  transfers between devices with their start and end apart: 12, of which 9 were waited for; matrix products, arithmetic and copies ran while one was open for 6% of the time, Pallas kernels for 0%

commit v1 on v0

--- a/solution.py
+++ b/solution.py
@@ -149,7 +149,7 @@
     d_pre_low = d_pre.astype(jnp.bfloat16)
     grad_up = jnp.einsum("td,tf->df", first_low, d_pre_low, preferred_element_type=jnp.float32)
     first_part = jnp.einsum("tf,df->td", d_pre_low, wide_up, preferred_element_type=jnp.float32)
-    d_first = lax.psum(first_part, "tensor") + d_second
+    d_first = jnp.sum(lax.all_gather(first_part, "tensor"), axis=0) + d_second
     grad_first_shift = jnp.sum(d_first, axis=0)
     grad_first_gain = jnp.sum(d_first * first_normed, axis=0)
     d_attn = norm_back(d_first, first_normed, first_inverse, first_gain)

time: 579 us -> 626 us (1.081)
  waiting for transfers between devices: 333 us -> 377 us
  matrix products: 38.8 us -> 45.9 us
    all_gather x0 -> x1, waiting for transfers between devices: none -> 114 us  [per_device(): d_first = jnp.sum(lax.all_gather(first_part, 'tensor'), axis=0) + d_second]
    psum x1 -> x0, waiting for transfers between devices: 67.4 us -> none  [per_device(): d_first = lax.psum(first_part, 'tensor') + d_second]
    unnamed x14, waiting for transfers between devices: 56.9 us -> 39.3 us
    reduce_scatter x1, waiting for transfers between devices: 13.2 us -> 27.5 us  [per_device(): lax.psum_scatter(local_grads[2], ('dp', 'ctx'), scatter_dimension=0, tile...]
    dynamic_update_slice x8, local copies, waits for them, and re-layouts: 33.7 us -> 25 us  [per_device(): lax.scan(back_block, jnp.zeros((row_count, heads_here, HD), jnp.float32),...]
    unnamed x89 -> x67, local copies, waits for them, and re-layouts: 19.3 us -> 24.4 us
where the time goes in v1:
time: 626 us; the launch traced here: 624 us
  waiting for transfers between devices  377 us (60%)
  blocking collectives  95.7 us (15%)
  local copies, waits for them, and re-layouts  60 us (10%)
  matrix products  45.9 us (7%)
  other arithmetic  25.5 us (4%)
  between operations  15.8 us (3%)
    all_gather x1, waiting for transfers between devices, per_device(): d_first = jnp.sum(lax.all_gather(first_part, 'tensor'), axis=0) + d_second  114 us
    psum x1, waiting for transfers between devices, per_device(): lax.psum(attn_part, 'tensor')  68.7 us
    psum x1, waiting for transfers between devices, per_device(): second_sum = first_out + lax.psum(down_part, 'tensor') + down_bias  68.2 us
    unnamed x14, waiting for transfers between devices  39.3 us
    reduce_scatter x1, waiting for transfers between devices, per_device(): lax.psum_scatter(local_grads[3], ('dp', 'ctx'), scatter_dimension=1, tile...  36.2 us
    reduce_scatter x1, waiting for transfers between devices, per_device(): lax.psum_scatter(local_grads[2], ('dp', 'ctx'), scatter_dimension=0, tile...  27.5 us
    dynamic_update_slice x8, local copies, waits for them, and re-layouts, per_device(): lax.scan(back_block, jnp.zeros((row_count, heads_here, HD), jnp.float32),...  25 us
    psum x1, blocking collectives, per_device(): lax.psum((grad_query_bias, grad_value_bias, grad_proj_bias, grad_first_ga...  24.9 us
  transfers between devices with their start and end apart: 12, of which 9 were waited for; matrix products, arithmetic and copies ran while one was open for 6% of the time, Pallas kernels for 0%

profile of v1, /device:TPU:0, one launch (start us, length us, event | category | flops | bytes accessed | tf_op | source)
XLA Modules:
  0.0 623.6 jit_solution(5150644758274349653)
XLA Ops:
  9.4 14.3 %all_gather.38 = bf16[3,768,192]{2,0,1:T(4,128)(2,1)S(1)} all-gather(bf16[3,192,192]{2,0,1:T(4,128)(2,1)S(1)} %copy.46), channel_id=1, replica_groups=mesh['dp'=4,'ctx'=2,'tensor'=4] {'dp'}, dimensions={1}, use_global_device_ids=true | all-gather | bytes 1105920 | tf_op jit(solution)/shard_map/all_gather | solution.py:96
  25.8 7.8 %all_gather.40 = bf16[1024,3,64]{0,2,1:T(8,128)(2,1)S(1)} all-gather(bf16[512,3,64]{0,2,1:T(8,128)(2,1)S(1)} %add_convert_fusion.1), channel_id=1, replica_groups=mesh['dp'=4,'ctx'=2,'tensor'=4] {'ctx'}, dimensions={0}, use_global_device_ids=true | all-gather | bytes 589824 | tf_op jit(solution)/shard_map/all_gather | solution.py:120
  34.5 7.0 %all_gather.39 = bf16[1024,3,64]{0,2,1:T(8,128)(2,1)S(1)} all-gather(bf16[512,3,64]{0,2,1:T(8,128)(2,1)S(1)} %bitcast.196), channel_id=1, replica_groups=mesh['dp'=4,'ctx'=2,'tensor'=4] {'ctx'}, dimensions={0}, use_global_device_ids=true | all-gather | bytes 589824 | tf_op jit(solution)/shard_map/all_gather | solution.py:119
  42.3 14.4 %while.30 = (s32[]{:T(128)}, f32[3,512]{1,0:T(4,128)S(1)}, f32[3,512]{1,0:T(4,128)S(1)}, f32[512,3,64]{0,2,1:T(8,128)}, s32[2]{0:T(128)S(1)}, /*index=5*/s32[]{:...) while((s32[]{:T(128)}, f32[3,512]{1,0:T(4,128)S(1)}, ...), condition=%wide.region_3.4_spmd.clone, body=%wide.region_0.3_spmd.clone.sunk | while | flops 211855360 | bytes 10919585 | solution.py:73
  56.8 6.1 all_gather.41
  66.8 68.7 %all-reduce.5.cloned.1.call-done = f32[512,768]{1,0:T(8,128)} async-done(((f32[512,768]{1,0:T(8,128)}), f32[512,768]{1,0:T(8,128)}) %all-reduce.5.cloned.1.call-update) | async-done | bytes 1572880 | tf_op jit(solution)/shard_map/psum | solution.py:130
  145.5 68.2 %all-reduce.7.cloned.1.call-done = f32[512,768]{1,0:T(8,128)} async-done(((f32[512,768]{1,0:T(8,128)}), f32[512,768]{1,0:T(8,128)}) %all-reduce.7.cloned.1.call-update) | async-done | bytes 1572880 | tf_op jit(solution)/shard_map/psum | solution.py:136
  224.0 114.4 %all-gather.9.cloned.1.call-done = f32[2048,768]{1,0:T(8,128)} async-done(((f32[512,768]{1,0:T(8,128)}), f32[2048,768]{1,0:T(8,128)}) %all-gather.9.cloned.1.call-update) | async-done | bytes 6291472 | tf_op jit(solution)/shard_map/all_gather | solution.py:152
  338.4 4.5 reduce_sum.190
  347.9 42.6 %while.31 = (s32[]{:T(128)}, f32[512,3,64]{0,2,1:T(8,128)S(1)}, f32[2,512,3,64]{1,0,3,2:T(2,128)}, f32[2,512,3,64]{1,0,3,2:T(2,128)}, bf16[2,512,3,64]{1,3,2,0:T...) while((s32[]{:T(128)}, f32[512,3,64]{0,2,1:T(8,128)S(1)}, ...), condition=%wide.region_17.18_spmd.clone, body=%wide.region_16.17_spmd.clone.sunk | while | flops 513147904 | bytes 40722232 | solution.py:206
  352.9 8.0 %dynamic_update_slice.11 = f32[2,512,3,64]{1,0,3,2:T(2,128)} dynamic-update-slice(f32[2,512,3,64]{1,0,3,2:T(2,128)} %get-tuple-element.565, f32[1,512,3,64]{1,0,3,2:T(1,128)S(1)} %copy.100, s32[]{:T(128)} %get-tuple-element.563, s32[]{:T(128)} %constant.61.clone.1..sunk.1, s32[]{:T(128)} %constant.61.clone.1..sunk.1, s32[]{:T(128)} %constant.61.clone.1..sunk.1) | dynamic-update-slice | bytes 786436 | tf_op jit(solution)/shard_map/while/body/jit(dynamic_update_index_in_dim)/dynamic_update_slice | solution.py:206
  374.2 8.0 %dynamic_update_slice.11 = f32[2,512,3,64]{1,0,3,2:T(2,128)} dynamic-update-slice(f32[2,512,3,64]{1,0,3,2:T(2,128)} %get-tuple-element.565, f32[1,512,3,64]{1,0,3,2:T(1,128)S(1)} %copy.100, s32[]{:T(128)} %get-tuple-element.563, s32[]{:T(128)} %constant.61.clone.1..sunk.1, s32[]{:T(128)} %constant.61.clone.1..sunk.1, s32[]{:T(128)} %constant.61.clone.1..sunk.1) | dynamic-update-slice | bytes 786436 | tf_op jit(solution)/shard_map/while/body/jit(dynamic_update_index_in_dim)/dynamic_update_slice | solution.py:206
  410.1 18.7 %reduce-scatter.13.cloned.1.call-done = f32[512,3,64]{0,2,1:T(8,128)} async-done(((f32[1024,3,64]{0,2,1:T(8,128)}), f32[512,3,64]{0,2,1:T(8,128)}) %reduce-scatter.13.cloned.1.call-update) | async-done | bytes 393232 | tf_op jit(solution)/shard_map/reduce_scatter | solution.py:213
  436.5 4.3 copy.61
  440.8 4.8 reshape.181
  446.8 27.5 %reduce-scatter.15.cloned.1.call-done = f32[96,768]{1,0:T(8,128)} async-done(((f32[768,768]{1,0:T(8,128)}), f32[96,768]{1,0:T(8,128)}) %reduce-scatter.15.cloned.1.call-update) | async-done | bytes 294928 | tf_op jit(solution)/shard_map/reduce_scatter | solution.py:234
  474.3 9.4 %all_gather.48 = f32[192,768]{1,0:T(8,128)S(1)} all-gather(f32[96,768]{1,0:T(8,128)} %reduce-scatter.15.cloned.1.call-done), channel_id=1, replica_groups=mesh['dp'=4,'ctx'=2,'tensor'=4] {'ctx'}, dimensions={0}, use_global_device_ids=true | all-gather | bytes 884736 | tf_op jit(solution)/shard_map/all_gather | solution.py:240
  483.8 36.2 %reduce-scatter.17.cloned.1.call-done = f32[768,96]{0,1:T(8,128)} async-done(((f32[768,768]{0,1:T(8,128)}), f32[768,96]{0,1:T(8,128)}) %reduce-scatter.17.cloned.1.call-update) | async-done | bytes 294928 | tf_op jit(solution)/shard_map/reduce_scatter | solution.py:235
  520.0 9.4 %all_gather.49 = f32[768,192]{0,1:T(8,128)S(1)} all-gather(f32[768,96]{0,1:T(8,128)} %reduce-scatter.17.cloned.1.call-done), channel_id=1, replica_groups=mesh['dp'=4,'ctx'=2,'tensor'=4] {'ctx'}, dimensions={1}, use_global_device_ids=true | all-gather | bytes 884736 | tf_op jit(solution)/shard_map/all_gather | solution.py:241
  529.4 28.5 %reduce-scatter.21.cloned.1.call-done = f32[96,192]{1,0:T(8,128)} async-done(((f32[768,192]{1,0:T(8,128)}), f32[96,192]{1,0:T(8,128)}) %reduce-scatter.21.cloned.1.call-update) | async-done | bytes 73744
  557.9 5.5 all_gather.47
  564.3 24.9 %all-reduce = (f32[192]{0:T(256)}, f32[192]{0:T(256)}, f32[768]{0:T(1024)}, f32[768]{0:T(1024)}, f32[768]{0:T(1024)}, /*index=5*/f32[768]{0:T(1024)}, f32[768]{0:T(1024)}, f32[768]{0:T(1024)}, f32[768]{0:T(1024)}) all-reduce(f32[192]{0:T(256)S(1)} %reduce_sum.195, ...), channel_id=1, replica_groups=mesh['dp'=4,'ctx'=2,'tensor'=4] {'dp','ctx'}, use_global_device_ids=true, to_apply=%region_23.24 | all-reduce | flops 5760 | bytes 46080 | tf_op jit(solution)/shard_map/psum | solution.py:243
  591.9 9.6 %reduce-scatter.19.cloned.1.call-done = f32[96,576]{1,0:T(8,128)} async-done(((f32[768,576]{1,0:T(8,128)}), f32[96,576]{1,0:T(8,128)}) %reduce-scatter.19.cloned.1.call-update) | async-done | bytes 221200
  602.7 11.3 %all_gather.46 = f32[3,192,192]{2,0,1:T(4,128)S(1)} all-gather(f32[3,96,192]{2,0,1:T(4,128)S(1)} %bitcast.193), channel_id=1, replica_groups=mesh['dp'=4,'ctx'=2,'tensor'=4] {'ctx'}, dimensions={1}, use_global_device_ids=true | all-gather | bytes 663552 | tf_op jit(solution)/shard_map/all_gather | solution.py:238
  (200 shorter events, 107.6 us)
Async XLA Ops:
  8.0 15.7 %copy-start.16 = (bf16[1,512,768]{2,1,0:T(8,128)(2,1)S(1)}, bf16[1,512,768]{2,1,0:T(8,128)(2,1)}, u32[]{:S(2)}) copy-start(bf16[1,512,768]{2,1,0:T(8,128)(2,1)} %param.20) | copy-start | bytes 2359300
  8.0 127.5 %all-reduce.5.cloned.1.call-start = ((), (), s32[]{:S(2)}) async-start(), calls=%async_computation.6 | async-start | bytes 3145728 | tf_op jit(solution)/shard_map/psum | solution.py:130
  25.0 9.4 %copy-start.27 = (f32[192]{0:T(256)S(1)}, f32[192]{0:T(256)}, u32[]{:S(2)}) copy-start(f32[192]{0:T(256)} %param.24) | copy-start | bytes 2308
  42.3 14.4 %copy-start.19 = (bf16[192,192]{1,0:T(8,128)(2,1)S(1)}, bf16[192,192]{1,0:T(8,128)(2,1)}, u32[]{:S(2)}) copy-start(bf16[192,192]{1,0:T(8,128)(2,1)} %param.26) | copy-start | bytes 221188
  65.6 70.0 %copy-start.22 = (f32[768]{0:T(1024)S(1)}, f32[768]{0:T(1024)}, u32[]{:S(2)}) copy-start(f32[768]{0:T(1024)} %param.27) | copy-start | bytes 9220
  65.6 72.2 %all-gather.5.cloned.1.call-start = ((), (), s32[]{:S(2)}) async-start(), calls=%async_computation.7 | async-start | bytes 1474560 | tf_op jit(solution)/shard_map/all_gather | solution.py:98
  66.2 75.8 %all-gather.7.cloned.1.call-start = ((), (), s32[]{:S(2)}) async-start(), calls=%async_computation.8 | async-start | bytes 1474560 | tf_op jit(solution)/shard_map/all_gather | solution.py:99
  66.8 147.0 %all-reduce.7.cloned.1.call-start = ((), (), s32[]{:S(2)}) async-start(), calls=%async_computation.9 | async-start | bytes 3145728 | tf_op jit(solution)/shard_map/psum | solution.py:136
  137.4 208.2 %copy-start.1 = (f32[512,768]{1,0:T(8,128)}, f32[512,768]{1,0:T(8,128)S(1)}, u32[]{:S(2)}) copy-start(f32[512,768]{1,0:T(8,128)S(1)} %get-tuple-element.358) | copy-start | bytes 4718596
  145.5 68.3 %copy-start.23 = (f32[768]{0:T(1024)S(1)}, f32[768]{0:T(1024)}, u32[]{:S(2)}) copy-start(f32[768]{0:T(1024)} %param.33) | copy-start | bytes 9220
  145.5 192.9 %all-gather.9.cloned.1.call-start = ((), (), s32[]{:S(2)}) async-start(), calls=%async_computation.15 | async-start | bytes 7864320 | tf_op jit(solution)/shard_map/all_gather | solution.py:152
  223.8 185.3 %reduce-scatter.11.cloned.1.call-start = ((), (), s32[]{:S(2)}) async-start(), calls=%async_computation.10 | async-start | bytes 1179648 | tf_op jit(solution)/shard_map/reduce_scatter | solution.py:212
  347.9 2.7 copy-start.18
  348.6 3.3 copy-start
  361.3 3.3 copy-start.13
  369.8 3.3 copy-start
  382.6 3.3 copy-start.13
  390.5 2.8 copy-start.15
  393.3 35.5 %reduce-scatter.13.cloned.1.call-start = ((), (), s32[]{:S(2)}) async-start(), calls=%async_computation.11 | async-start | bytes 1179648 | tf_op jit(solution)/shard_map/reduce_scatter | solution.py:213
  395.0 79.4 %reduce-scatter.15.cloned.1.call-start = ((), (), s32[]{:S(2)}) async-start(), calls=%async_computation.13 | async-start | bytes 2654208 | tf_op jit(solution)/shard_map/reduce_scatter | solution.py:234
  398.6 121.3 %reduce-scatter.17.cloned.1.call-start = ((), (), s32[]{:S(2)}) async-start(), calls=%async_computation.14 | async-start | bytes 2654208 | tf_op jit(solution)/shard_map/reduce_scatter | solution.py:235
  402.5 155.4 %reduce-scatter.21.cloned.1.call-start = ((), (), s32[]{:S(2)}) async-start(), calls=%async_computation.17 | async-start | bytes 884736
  405.2 183.9 %all-reduce.9.cloned.1.call-start = ((), (), s32[]{:S(2)}) async-start(), calls=%async_computation.12 | async-start | bytes 3145728 | tf_op jit(solution)/shard_map/psum | solution.py:229
  433.4 168.1 %reduce-scatter.19.cloned.1.call-start = ((), (), s32[]{:S(2)}) async-start(), calls=%async_computation.16 | async-start | bytes 2211840
  (25 other events, 33.5 us)
Sparse Core Ops, SparseCore 0:
  65.7 69.7 all-reduce.4
  145.6 68.1 all-reduce.6
  223.9 114.4 all-gather.8
  433.5 68.9 all-reduce.8
Sparse Core Ops, SparseCore 1:
  67.6 18.1 all-gather.4
  87.2 17.3 all-gather.6
  393.4 15.6 reduce-scatter.10
  411.3 17.4 reduce-scatter.12
  432.1 42.1 reduce-scatter.14
  477.7 42.2 reduce-scatter.16
  523.0 34.9 reduce-scatter.20
  561.2 40.3 reduce-scatter.18
